TPU v7x, 32 devices: a whole 2x2x4 slice. The times are simulated.
32 devices in a mesh: section: 2 (over core), tensor: 2 (over x), dp: 8 (over z, y).
Axes of the slice: x: 2, y: 2, z: 4, core: 2. Of those that a mesh axis runs over, the one named last changes fastest.
Arguments:
- exit_hidden: bfloat16 [64, 4, 2048], P('dp', None, ('section', 'tensor')), may hold values from -6 to 6
- exit_depth: int32 [64], P('dp'), may hold values from 0 to 1, as said below
- context_len: int32 [64], P('dp'), may hold values from 48 to 384
- attn_gain: float32 [2, 2048], P('section'), may hold values from 0.1 to 1.9
- w_query: bfloat16 [2, 2048, 2048], P('section', None, 'tensor'), may hold values from -0.125 to 0.125
- w_keyval: bfloat16 [2, 2048, 1024], P('section', None, 'tensor'), may hold values from -0.125 to 0.125
- w_out: bfloat16 [2, 2048, 2048], P('section', 'tensor'), may hold values from -0.125 to 0.125
- kv_cache: bfloat16 [2, 64, 384, 8, 128], P('section', 'dp', None, 'tensor'), may hold values from -400 to 400
- mlp_gain: float32 [2, 2048], P('section'), may hold values from 0.1 to 1.9
- w_gate: bfloat16 [2, 2048, 4096], P('section', 'dp', 'tensor'), may hold values from -0.125 to 0.125
- w_up: bfloat16 [2, 2048, 4096], P('section', 'dp', 'tensor'), may hold values from -0.125 to 0.125
- w_down: bfloat16 [2, 2048, 4096], P('section', 'dp', 'tensor'), may hold values from -0.09375 to 0.09375
Outputs:
- layer_states: bfloat16 [2, 64, 4, 2048], P('section', 'dp', None, 'tensor')
Inputs may be any that keep to these rules, and one draw needn't show every extreme that they name: `exit_depth`: every depth from 0 to 1 is held by some request.
All inputs are finite; a program needn't handle non-finite values.
Results may differ from a plain program's by a relative error of at most 0.019.
Values may be sent and summed in bfloat16 or wider, within the bound.
A program may use at most 192 MiB of HBM per device.

v0:
```python
import math

import jax
import jax.numpy as jnp
from jax import lax
from jax.sharding import PartitionSpec as P

D = 2048
DRAFT = 4
CTX = 384
R_DEV = 8


EPS = 1e-05
THETA = 500000.0
NEGATIVE = -1e30


def shifted(array, axis, by):
    length = lax.axis_size(axis)
    pairs = [(i, i + by) for i in range(length) if 0 <= i + by < length]
    return lax.ppermute(array, axis, pairs)


def rotate(values, where_at):
    middle = values.shape[-1] // 2
    rates = jnp.exp(
        jnp.arange(middle, dtype=jnp.float32) * (-2.0 * math.log(THETA) / values.shape[-1])
    )
    angles = where_at.astype(jnp.float32)[..., None] * rates
    cosine = jnp.cos(angles)
    sine = jnp.sin(angles)
    first = values[..., :middle]
    second = values[..., middle:]
    return jnp.concatenate(
        [first * cosine - second * sine, second * cosine + first * sine], axis=-1
    )


def normalize(hidden, gain):
    wide = hidden.astype(jnp.float32)
    factor = lax.rsqrt(jnp.mean(wide * wide, axis=-1, keepdims=True) + EPS)
    return (wide * factor * gain).astype(jnp.bfloat16)


def attend(normed, lengths, cache, w_query, w_keyval, w_out):
    rows, drafts, width = normed.shape
    head_size = cache.shape[-1] // 2
    kv_count = cache.shape[2]
    q_count = w_query.shape[-1] // head_size
    group = q_count // kv_count
    flat = normed.reshape(rows * drafts, width)
    query = jnp.dot(flat, w_query, preferred_element_type=jnp.float32).reshape(
        rows, drafts, kv_count, group, head_size
    )
    keyval = jnp.dot(flat, w_keyval, preferred_element_type=jnp.float32).reshape(
        rows, drafts, kv_count, 2 * head_size
    )
    places = lengths[:, None] + jnp.arange(drafts, dtype=jnp.int32)[None, :]
    query = rotate(query, places[:, :, None, None]).astype(jnp.bfloat16)
    fresh_keys = rotate(keyval[..., :head_size], places[:, :, None]).astype(jnp.bfloat16)
    fresh_values = keyval[..., head_size:].astype(jnp.bfloat16)
    cached_keys = cache[..., :head_size]
    cached_values = cache[..., head_size:]
    scale = head_size ** (-0.5)
    old_scores = (
        jnp.einsum("rjkgd,rpkd->rkgjp", query, cached_keys, preferred_element_type=jnp.float32)
        * scale
    )
    live = jnp.arange(cache.shape[1], dtype=jnp.int32)[None, :] < lengths[:, None]
    old_scores = jnp.where(live[:, None, None, None, :], old_scores, NEGATIVE)
    new_scores = (
        jnp.einsum("rjkgd,rikd->rkgji", query, fresh_keys, preferred_element_type=jnp.float32)
        * scale
    )
    causal = jnp.arange(drafts)[None, :] <= jnp.arange(drafts)[:, None]
    new_scores = jnp.where(causal, new_scores, NEGATIVE)
    top = jnp.maximum(old_scores.max(axis=-1), new_scores.max(axis=-1))[..., None]
    old_weights = jnp.exp(old_scores - top)
    new_weights = jnp.exp(new_scores - top)
    total = old_weights.sum(axis=-1, keepdims=True) + new_weights.sum(axis=-1, keepdims=True)
    old_weights = (old_weights / total).astype(jnp.bfloat16)
    new_weights = (new_weights / total).astype(jnp.bfloat16)
    mixed = jnp.einsum(
        "rkgjp,rpkd->rjkgd", old_weights, cached_values, preferred_element_type=jnp.float32
    )
    mixed = mixed + jnp.einsum(
        "rkgji,rikd->rjkgd", new_weights, fresh_values, preferred_element_type=jnp.float32
    )
    heads_out = mixed.astype(jnp.bfloat16).reshape(rows * drafts, q_count * head_size)
    return jnp.dot(heads_out, w_out, preferred_element_type=jnp.float32)


def feed_forward(normed, gate_full, up_full, down_full):
    flat = normed.reshape(-1, normed.shape[-1])
    gate = jnp.dot(flat, gate_full, preferred_element_type=jnp.float32)
    up = jnp.dot(flat, up_full, preferred_element_type=jnp.float32)
    act = (jax.nn.silu(gate) * up).astype(jnp.bfloat16)
    return lax.dot_general(
        act, down_full, (((1,), (1,)), ((), ())), preferred_element_type=jnp.float32
    )


def local(
    exit_hidden,
    exit_depth,
    context_len,
    attn_gain,
    w_query,
    w_keyval,
    w_out,
    kv_cache,
    mlp_gain,
    w_gate,
    w_up,
    w_down,
):
    entry = lax.all_gather(exit_hidden, ("section", "tensor"), axis=2, tiled=True)
    gate_full, up_full, down_full = (
        lax.all_gather(w_gate[0], "dp", axis=0, tiled=True),
        lax.all_gather(w_up[0], "dp", axis=0, tiled=True),
        lax.all_gather(w_down[0], "dp", axis=0, tiled=True),
    )
    section = lax.axis_index("section")
    sections = lax.axis_size("section")
    pieces = 1
    members = R_DEV // pieces
    share = D // lax.axis_size("tensor")
    offset = lax.axis_index("tensor") * share
    entry = entry.reshape(pieces, members, DRAFT, D)
    depth = exit_depth.reshape(pieces, members)
    length = context_len.reshape(pieces, members)
    cache = kv_cache[0].reshape(pieces, members, CTX, kv_cache.shape[3], kv_cache.shape[4])
    gain = attn_gain[0]
    second_gain = mlp_gain[0]
    query_weight = w_query[0]
    keyval_weight = w_keyval[0]
    out_weight = w_out[0]

    def turn_step(turn, carry):
        received, outputs = carry
        block = turn - section
        valid = (block >= 0) & (block < pieces)
        index = jnp.clip(block, 0, pieces - 1)
        block_depth = depth[index]
        block_length = length[index]
        block_entry = entry[index]
        block_cache = cache[index]
        take = (block_depth >= section)[:, None, None]
        keep = (block_depth <= section)[:, None, None]
        active = valid & jnp.any(block_depth <= section)

        def compute(whole):
            return attend(
                normalize(whole, gain),
                block_length,
                block_cache,
                query_weight,
                keyval_weight,
                out_weight,
            )

        def branch_work(middle):
            return feed_forward(normalize(middle, second_gain), gate_full, up_full, down_full)

        def skipped(whole):
            return jnp.zeros((members * DRAFT, D), jnp.float32)

        whole = jnp.where(take, block_entry, received)
        partial_value = lax.cond(active, compute, skipped, whole)
        summed = lax.psum(partial_value, "tensor").reshape(members, DRAFT, D)
        middle = (whole.astype(jnp.float32) + summed).astype(jnp.bfloat16)
        branch = lax.cond(active, branch_work, skipped, middle)
        branch_sum = (
            lax.psum(branch.astype(jnp.bfloat16), "tensor")
            .astype(jnp.float32)
            .reshape(members, DRAFT, D)
        )
        updated = (middle.astype(jnp.float32) + branch_sum).astype(jnp.bfloat16)
        result = jnp.where(keep, updated, whole)
        own = lax.dynamic_slice_in_dim(result, offset, share, 2)
        stored = jnp.where(valid, own, outputs[index])
        outputs = lax.dynamic_update_index_in_dim(outputs, stored, index, 0)
        received = shifted(result, "section", 1)
        return (received, outputs)

    carried = D
    start = (
        jnp.zeros((members, DRAFT, carried), jnp.bfloat16),
        jnp.zeros((pieces, members, DRAFT, share), jnp.bfloat16),
    )
    final = lax.fori_loop(0, sections + pieces - 1, turn_step, start)
    return final[1]


def solution(mesh):
    in_specs = (
        P("dp", None, ("section", "tensor")),
        P("dp"),
        P("dp"),
        P("section", None),
        P("section", None, "tensor"),
        P("section", None, "tensor"),
        P("section", "tensor", None),
        P("section", "dp", None, "tensor", None),
        P("section", None),
        P("section", "dp", "tensor"),
        P("section", "dp", "tensor"),
        P("section", "dp", "tensor"),
    )
    out_specs = P("section", "dp", None, "tensor")
    return jax.shard_map(local, mesh=mesh, in_specs=in_specs, out_specs=out_specs, check_vma=False)
```

profile of v0, /device:TPU:3, one launch (start us, length us, event | category | flops | bytes accessed | tf_op | source)
XLA Modules:
  0.0 560.0 jit_solution(6729195397710734736)
XLA Ops:
  6.5 0.7 all-gather.7.cloned.1.call-update
  7.3 0.7 all-gather.9.cloned.1.call-update
  8.1 0.7 all-gather.11.cloned.1.call-update
  8.8 6.6 %copy.31 = bf16[1,2048,1024]{1,2,0:T(8,128)(2,1)} copy(bf16[1,2048,1024]{2,1,0:T(8,128)(2,1)} %param.22) | data formatting | bytes 8388608 | tf_op args[4]
  15.4 3.5 copy.33
  19.0 3.1 copy.32
  22.1 10.2 %all_gather.12 = bf16[8,4,2048]{2,1,0:T(4,128)(2,1)S(1)} all-gather(bf16[8,4,512]{2,1,0:T(4,128)(2,1)S(1)} %copy-done.7), channel_id=1, replica_groups=mesh['section'=2,'tensor'=2,'dp'=8] {'section','tensor'}, dimensions={2}, use_global_device_ids=true | all-gather | bytes 163840 | tf_op jit(solution)/shard_map/all_gather | solution.py:118
  32.3 0.7 compare_reduce_fusion
  33.0 101.5 %all-gather.7.cloned.1.call-done = bf16[1,2048,2048]{2,1,0:T(8,128)(2,1)} async-done(((bf16[1,256,2048]{2,1,0:T(8,128)(2,1)}), bf16[1,2048,2048]{2,1,0:T(8,128)(2,1)}) %all-gather.7.cloned.1.call-update) | async-done | bytes 8388624 | tf_op jit(solution)/shard_map/all_gather | solution.py:120
  134.5 124.8 %all-gather.9.cloned.1.call-done = bf16[1,2048,2048]{2,1,0:T(8,128)(2,1)} async-done(((bf16[1,256,2048]{2,1,0:T(8,128)(2,1)}), bf16[1,2048,2048]{2,1,0:T(8,128)(2,1)}) %all-gather.9.cloned.1.call-update) | async-done | bytes 8388624 | tf_op jit(solution)/shard_map/all_gather | solution.py:121
  259.3 124.8 %all-gather.11.cloned.1.call-done = bf16[1,2048,2048]{2,1,0:T(8,128)(2,1)} async-done(((bf16[1,256,2048]{2,1,0:T(8,128)(2,1)}), bf16[1,2048,2048]{2,1,0:T(8,128)(2,1)}) %all-gather.11.cloned.1.call-update) | async-done | bytes 8388624 | tf_op jit(solution)/shard_map/all_gather | solution.py:122
  384.2 168.3 %while.18 = (s32[]{:T(128)}, bf16[8,4,2048]{2,1,0:T(4,128)(2,1)S(1)}, bf16[1,8,4,1024]{3,2,1,0:T(4,128)(2,1)S(1)}, s32[]{:T(128)}, s32[1,8]{1,0:T(1,128)S(1)}, /...) while((s32[]{:T(128)}, ...), condition=%wide.region_14.15_spmd, body=%wide.region_1.14_spmd.sunk | while | flops 1196018816 | bytes 63734276 | solution.py:192
  384.3 0.6 compare_bitcast_fusion.3
  385.7 0.8 reshape.236
  386.6 39.0 %all-reduce.3.cloned.1.call-done = f32[8,4,2048]{2,1,0:T(4,128)} async-done(((f32[8,4,2048]{2,1,0:T(4,128)}), f32[8,4,2048]{2,1,0:T(4,128)}) %all-reduce.3.cloned.1.call-update) | async-done | bytes 262160 | tf_op jit(solution)/shard_map/while/body/eval_jaxpr/psum | solution.py:171
  425.5 1.0 add_convert_fusion.6
  426.6 0.7 reshape.237
  427.4 36.3 %all-reduce.5.cloned.1.call-done = bf16[8,4,2048]{2,1,0:T(4,128)(2,1)} async-done(((bf16[8,4,2048]{2,1,0:T(4,128)(2,1)}), bf16[8,4,2048]{2,1,0:T(4,128)(2,1)}) %all-reduce.5.cloned.1.call-update) | async-done | bytes 131088 | tf_op jit(solution)/shard_map/while/body/eval_jaxpr/psum | solution.py:175
  463.7 1.1 fusion.57
  464.7 1.3 collective-permute-start
  466.1 1.9 collective-permute-done
  468.0 0.6 compare_bitcast_fusion.3
  469.4 17.9 %conditional.4 = (f32[32,2048]{1,0:T(8,128)S(1)}) conditional(s32[]{:T(128)} %convert_element_type.166, () %tuple.68, (s32[1,8]{1,0:T(1,128)}, bf16[8,4,2048]{2,1,0:T(4,128)(2,1)S(1)}, f32[1,2048]{1,0:T(1,128)S(1)}, bf16[2048,1024]{0,1:T(8,128)(2,1)}, bf16[1,8,384,4,128]{2,4,3,1,0:T(8,128)(2,1)}, /*index=5*/bf16[2048,512]{0,1:T(8,128)(2,1)S(1)}, ...), branch_computations={%region_2.2_spmd, %region_3.8_spmd} | conditional | flops 389106816 | bytes 31677728 | solution.py:170
  469.4 0.2 fusion.12
  469.6 0.7 fusion.16
  470.4 0.7 add_convert_fusion.2
  471.4 4.4 fusion.18
  476.1 1.3 fusion.42
  477.3 0.7 iota_compare_fusion
  478.1 0.6 fusion.41
  478.7 0.3 fusion.15
  478.9 0.6 fusion.10
  479.7 1.6 copy.28
  481.3 0.4 divide_convert_fusion
  481.6 2.1 fusion.8
  484.3 3.0 fusion.44
  487.3 0.8 reshape.236
  488.1 22.9 %all-reduce.3.cloned.1.call-done = f32[8,4,2048]{2,1,0:T(4,128)} async-done(((f32[8,4,2048]{2,1,0:T(4,128)}), f32[8,4,2048]{2,1,0:T(4,128)}) %all-reduce.3.cloned.1.call-update) | async-done | bytes 262160 | tf_op jit(solution)/shard_map/while/body/eval_jaxpr/psum | solution.py:171
  511.1 1.0 add_convert_fusion.6
  512.1 15.1 %conditional.5 = (bf16[32,2048]{1,0:T(8,128)(2,1)S(1)}) conditional(s32[]{:T(128)} %convert_element_type.166, () %tuple.67, (bf16[8,4,2048]{2,1,0:T(4,128)(2,1)S(1)}, f32[1,2048]{1,0:T(1,128)S(1)}, bf16[2048,2048]{1,0:T(8,128)(2,1)}, bf16[2048,2048]{1,0:T(8,128)(2,1)}, bf16[2048,2048]{1,0:T(8,128)(2,1)}) %tuple.70), branch_computations={%region_10.10_spmd, %region_11.12_spmd} | conditional | flops 806158336 | bytes 26747400 | solution.py:173
  512.5 4.9 fusion.43
  517.4 9.8 %fusion.28 = bf16[32,2048]{1,0:T(8,128)(2,1)S(1)} fusion(bf16[2048,2048]{1,0:T(8,128)(2,1)} %get-tuple-element.508, bf16[32,2048]{1,0:T(8,128)(2,1)S(1)} %reshape.208, bf16[2048,2048]{1,0:T(8,128)(2,1)} %get-tuple-element.507, f32[32,2048]{1,0:T(8,128)S(1)} %fusion.43), kind=kOutput, calls=%fused_computation.51 | convolution fusion | flops 537264128 | bytes 17301504 | tf_op jit(solution)/shard_map/while/body/eval_jaxpr/cond/branch_1_fun/dot_general | solution.py:99
  527.3 0.7 reshape.237
  528.0 20.1 %all-reduce.5.cloned.1.call-done = bf16[8,4,2048]{2,1,0:T(4,128)(2,1)} async-done(((bf16[8,4,2048]{2,1,0:T(4,128)(2,1)}), bf16[8,4,2048]{2,1,0:T(4,128)(2,1)}) %all-reduce.5.cloned.1.call-update) | async-done | bytes 131088 | tf_op jit(solution)/shard_map/while/body/eval_jaxpr/psum | solution.py:175
  548.1 1.1 fusion.57
  549.2 1.3 collective-permute-start
  550.6 1.9 collective-permute-done
  552.5 0.6 copy-done.3
  (63 shorter events, 2.6 us)
Async XLA Ops:
  6.5 127.9 %all-gather.7.cloned.1.call-start = ((), (), s32[]{:S(2)}) async-start(), calls=%async_computation | async-start | bytes 9437184 | tf_op jit(solution)/shard_map/all_gather | solution.py:120
  7.3 252.0 %all-gather.9.cloned.1.call-start = ((), (), s32[]{:S(2)}) async-start(), calls=%async_computation.1 | async-start | bytes 9437184 | tf_op jit(solution)/shard_map/all_gather | solution.py:121
  8.0 376.1 %all-gather.11.cloned.1.call-start = ((), (), s32[]{:S(2)}) async-start(), calls=%async_computation.2 | async-start | bytes 9437184 | tf_op jit(solution)/shard_map/all_gather | solution.py:122
  8.8 6.7 %copy-start.1 = (bf16[1,8,384,4,128]{4,3,2,1,0:T(4,128)(2,1)S(1)}, bf16[1,8,384,4,128]{4,3,2,1,0:T(4,128)(2,1)}, u32[]{:S(2)}) copy-start(bf16[1,8,384,4,128]{4,3,2,1,0:T(4,128)(2,1)} %param.25) | copy-start | bytes 9437188
  15.4 6.7 %copy-start.7 = (bf16[8,4,512]{2,1,0:T(4,128)(2,1)S(1)}, bf16[8,4,512]{2,1,0:T(4,128)(2,1)}, u32[]{:S(2)}) copy-start(bf16[8,4,512]{2,1,0:T(4,128)(2,1)} %param.18) | copy-start | bytes 98308
  15.4 16.9 %copy-start.8 = (s32[8]{0:T(128)S(1)}, s32[8]{0:T(128)}, u32[]{:S(2)}) copy-start(s32[8]{0:T(128)} %param.19) | copy-start | bytes 100
  15.4 368.8 %copy-start.4 = (f32[1,2048]{1,0:T(1,128)S(1)}, f32[1,2048]{1,0:T(1,128)}, u32[]{:S(2)}) copy-start(f32[1,2048]{1,0:T(1,128)} %param.21) | copy-start | bytes 24580
  15.4 368.8 %copy-start.5 = (f32[1,2048]{1,0:T(1,128)S(1)}, f32[1,2048]{1,0:T(1,128)}, u32[]{:S(2)}) copy-start(f32[1,2048]{1,0:T(1,128)} %param.26) | copy-start | bytes 24580
  384.2 41.3 %all-reduce.3.cloned.1.call-start = ((), (), s32[]{:S(2)}) async-start(), calls=%async_computation.3 | async-start | bytes 524288 | tf_op jit(solution)/shard_map/while/body/eval_jaxpr/psum | solution.py:171
  386.5 77.1 %all-reduce.5.cloned.1.call-start = ((), (), s32[]{:S(2)}) async-start(), calls=%async_computation.4 | async-start | bytes 262144 | tf_op jit(solution)/shard_map/while/body/eval_jaxpr/psum | solution.py:175
  426.6 37.1 %copy-start.6 = (pred[8]{0:T(512)(128)(4,1)S(1)}, pred[8]{0:T(512)(128)(4,1)}, u32[]{:S(2)}) copy-start(pred[8]{0:T(512)(128)(4,1)} %get-tuple-element.740) | copy-start | bytes 28 | tf_op jit(solution)/shard_map/while
  426.6 41.4 %copy-start.9 = (s32[8]{0:T(128)S(1)}, s32[8]{0:T(128)}, u32[]{:S(2)}) copy-start(s32[8]{0:T(128)} %get-tuple-element.865) | copy-start | bytes 100 | tf_op jit(solution)/shard_map/while
  464.7 3.2 collective-permute-start
  468.0 43.1 %all-reduce.3.cloned.1.call-start = ((), (), s32[]{:S(2)}) async-start(), calls=%async_computation.3 | async-start | bytes 524288 | tf_op jit(solution)/shard_map/while/body/eval_jaxpr/psum | solution.py:171
  471.4 6.7 %copy-start.2 = (bf16[1,8,384,4,128]{2,4,3,1,0:T(8,128)(2,1)S(1)}, bf16[1,8,384,4,128]{2,4,3,1,0:T(8,128)(2,1)}, u32[]{:S(2)}) copy-start(bf16[1,8,384,4,128]{2,4,3,1,0:T(8,128)(2,1)} %get-tuple-element.501) | copy-start | bytes 9437188 | tf_op jit(solution)/shard_map/while/body/eval_jaxpr/cond
  481.3 2.6 copy-start
  488.1 60.0 %all-reduce.5.cloned.1.call-start = ((), (), s32[]{:S(2)}) async-start(), calls=%async_computation.4 | async-start | bytes 262144 | tf_op jit(solution)/shard_map/while/body/eval_jaxpr/psum | solution.py:175
  512.1 36.0 %copy-start.6 = (pred[8]{0:T(512)(128)(4,1)S(1)}, pred[8]{0:T(512)(128)(4,1)}, u32[]{:S(2)}) copy-start(pred[8]{0:T(512)(128)(4,1)} %get-tuple-element.740) | copy-start | bytes 28 | tf_op jit(solution)/shard_map/while
  512.1 40.4 %copy-start.9 = (s32[8]{0:T(128)S(1)}, s32[8]{0:T(128)}, u32[]{:S(2)}) copy-start(s32[8]{0:T(128)} %get-tuple-element.865) | copy-start | bytes 100 | tf_op jit(solution)/shard_map/while
  549.2 3.2 collective-permute-start
  552.5 0.6 copy-start.3
Sparse Core Ops, SparseCore 0:
  9.5 124.9 all-gather.6
  136.6 122.6 all-gather.8
  261.4 122.6 all-gather.10
  387.0 38.5 all-reduce.2
  427.6 35.9 all-reduce.4
  488.2 22.8 all-reduce.2
  528.1 19.9 all-reduce.4
where the time goes:
time: 563 us; the launch traced here: 560 us
  waiting for transfers between devices  475 us (84%)
  matrix products  27 us (5%)
  local copies, waits for them, and re-layouts  18.9 us (3%)
  between operations  13.5 us (2%)
  other arithmetic  10.5 us (2%)
  blocking collectives  10.2 us (2%)
    all_gather x1, waiting for transfers between devices, local(): lax.all_gather(w_down[0], 'dp', axis=0, tiled=True)  125 us
    all_gather x1, waiting for transfers between devices, local(): lax.all_gather(w_up[0], 'dp', axis=0, tiled=True)  125 us
    all_gather x1, waiting for transfers between devices, local(): lax.all_gather(w_gate[0], 'dp', axis=0, tiled=True)  102 us
    psum x2, waiting for transfers between devices, turn_step(): summed = lax.psum(partial_value, 'tensor').reshape(members, DRAFT, D)  61.9 us
    psum x2, waiting for transfers between devices, turn_step(): lax.psum(branch.astype(jnp.bfloat16), 'tensor').astype(jnp.float32)  56.4 us
  transfers between devices with their start and end apart: 9, of which 9 were waited for; matrix products, arithmetic and copies ran while one was open for 3% of the time, Pallas kernels for 0%

commit v1 on v0

--- a/solution.py
+++ b/solution.py
@@ -1,8 +1,12 @@
 import math
+
+import functools
 
 import jax
 import jax.numpy as jnp
 from jax import lax
+from jax.experimental import pallas as pl
+from jax.experimental.pallas import tpu as pltpu
 from jax.sharding import PartitionSpec as P
 
 D = 2048
@@ -193,6 +197,467 @@
     return final[1]
 
 
+MESH = pl.DeviceIdType.MESH
+BF = jnp.bfloat16
+F32 = jnp.float32
+
+
+def bits(size):
+    return size.bit_length() - 1
+
+
+def mm(a, b):
+    return jnp.dot(a, b, preferred_element_type=F32)
+
+
+def mm_t(a, b):
+    return lax.dot_general(a, b, (((1,), (1,)), ((), ())), preferred_element_type=F32)
+
+
+def lanes_like(shape):
+    return lax.broadcasted_iota(jnp.int32, shape, len(shape) - 1)
+
+
+def fused_kernel(
+    ndp,
+    lens_ref,
+    depth_ref,
+    cos_ref,
+    sin_ref,
+    gain_ref,
+    gain2_ref,
+    entry_ref,
+    wq_hbm,
+    wkv_hbm,
+    kv_hbm,
+    wo_hbm,
+    wg_hbm,
+    wu_hbm,
+    wd_hbm,
+    out_ref,
+    wq, wkv, kv, wo, wg, wu, wd,
+    ent, cur, whb, qs, kvs, qp, ns, oh, heads,
+    p1, mids, mid, xs, sqs, sqr,
+    ybuf, yrec, acc, zbuf, zrec, acts, fbuf, fin, res,
+    ld_sem, ent_s, ent_r, a_s, a_r, q_s, q_r, y_s, y_r, z_s, z_r,
+    g_s, g_r, h_s, f_s, f_r, c_s, c_r,
+):
+    s = lax.axis_index("section")
+    t = lax.axis_index("tensor")
+    d = lax.axis_index("dp")
+    half = ndp // 2
+    z = d // 2
+    y = d % 2
+    tok, width = cos_ref.shape[0], gain_ref.shape[1]
+    fb = width // ndp
+    reqs = lens_ref.shape[0]
+    drafts = tok // reqs
+    n_heads = wq.shape[1] // 64
+    n_kv = wkv.shape[1] // 128
+    ff = wg.shape[1]
+    rows = n_heads * drafts
+
+    loads = [
+        pltpu.make_async_copy(src, dst, ld_sem.at[i])
+        for i, (src, dst) in enumerate(
+            [(wq_hbm, wq), (wkv_hbm, wkv), (kv_hbm, kv), (wo_hbm, wo), (wg_hbm, wg), (wu_hbm, wu), (wd_hbm, wd)]
+        )
+    ]
+    for one in loads:
+        one.start()
+
+    barrier = pltpu.get_barrier_semaphore()
+    for k in range(1, 2 * ndp):
+        peer = (t * ndp + d + k) % (2 * ndp)
+        pl.semaphore_signal(barrier, inc=1, device_id=(s, peer // ndp, peer % ndp), device_id_type=MESH)
+    for k in range(2):
+        pl.semaphore_signal(barrier, inc=1, device_id=(1 - s, k, d), device_id_type=MESH)
+    pl.semaphore_wait(barrier, 2 * ndp + 1)
+
+    def remote(src, dst, send, recv, where):
+        return pltpu.make_async_remote_copy(
+            src_ref=src, dst_ref=dst, send_sem=send, recv_sem=recv, device_id=where, device_id_type=MESH
+        )
+
+    mine = s * 2 + t
+    pending = []
+    for k in range(1, 4):
+        other = (mine + k) % 4
+        copy = remote(entry_ref, ent.at[mine], ent_s.at[k - 1], ent_r.at[mine], (other // 2, other % 2, d))
+        copy.start()
+        pending.append(copy)
+    ent[mine] = entry_ref[...]
+
+    def permutation(transposed):
+        i = lax.broadcasted_iota(jnp.int32, (n_heads * tok,) * 2, 1 if transposed else 0)
+        c = lax.broadcasted_iota(jnp.int32, (n_heads * tok,) * 2, 0 if transposed else 1)
+        bd, bt, br = bits(drafts), bits(tok), bits(rows)
+        target = ((i & (rows - 1)) >> bd << bt) + (i >> br << bd) + (i & (drafts - 1))
+        return jnp.where(target == c, 1.0, 0.0).astype(BF)
+
+    for k in range(1, 4):
+        other = (mine + k) % 4
+        remote(entry_ref, ent.at[other], ent_s.at[k - 1], ent_r.at[other], (other // 2, other % 2, d)).wait_recv()
+
+    @pl.when(s == 0)
+    def _():
+        cur[...] = jnp.zeros_like(cur)
+
+    @pl.when(s == 1)
+    def _():
+        for k in range(2):
+            remote(res, cur.at[k], c_s.at[k], c_r.at[k], (0, k, d)).wait_recv()
+
+    depth = depth_ref[...][:, :1]
+    take = depth >= s
+    keep = depth <= s
+    wide = []
+    total_sq = None
+    per_ent = ent.shape[2] // fb
+    per_cur = cur.shape[2] // fb
+    for b in range(ndp):
+        e = ent[b // per_ent, :, (b % per_ent) * fb : (b % per_ent + 1) * fb].astype(F32)
+        c = cur[b // per_cur, :, (b % per_cur) * fb : (b % per_cur + 1) * fb].astype(F32)
+        w = jnp.where(take, e, c)
+        whb[b] = w.astype(BF)
+        wide.append(w)
+        sq = jnp.sum(w * w, axis=-1, keepdims=True)
+        total_sq = sq if total_sq is None else total_sq + sq
+    factor = lax.rsqrt(total_sq * (1.0 / width) + EPS)
+    normed = jnp.concatenate(
+        [(w * factor * gain_ref[:, b * fb : (b + 1) * fb]).astype(BF) for b, w in enumerate(wide)], axis=1
+    )
+
+    loads[0].wait()
+    for i in range(wq.shape[1] // 256):
+        qs[:, i * 256 : (i + 1) * 256] = mm(normed, wq[:, i * 256 : (i + 1) * 256])
+    loads[1].wait()
+    for i in range(wkv.shape[1] // 256):
+        kvs[:, i * 256 : (i + 1) * 256] = mm(normed, wkv[:, i * 256 : (i + 1) * 256])
+
+    cosine = cos_ref[...]
+    sine = sin_ref[...]
+    lane = lanes_like((tok, 128))
+    low = (lane & 63) < 32
+    left = lane < 64
+
+    def turned(x):
+        partner = jnp.where(low, pltpu.roll(x, 96, 1), pltpu.roll(x, 32, 1))
+        return x * cosine + partner * sine
+
+    stacked = []
+    for b in range(n_heads // 2):
+        x = turned(qs[:, b * 128 : (b + 1) * 128]) * (64 ** -0.5)
+        stacked.append(jnp.where(left, x, 0.0).astype(BF))
+        stacked.append(jnp.where(left, pltpu.roll(x, 64, 1), 0.0).astype(BF))
+    qp[...] = mm(permutation(False), jnp.concatenate(stacked, axis=0)).astype(BF)
+    fresh = []
+    for h in range(n_kv):
+        x = kvs[:, h * 128 : (h + 1) * 128]
+        fresh.append(jnp.where(left, turned(x), x).astype(BF))
+    fresh = jnp.concatenate(fresh, axis=0)
+
+    ri = lax.broadcasted_iota(jnp.int32, (reqs * rows, n_kv * tok), 0)
+    ci = lax.broadcasted_iota(jnp.int32, (reqs * rows, n_kv * tok), 1)
+    bg = bits(rows // n_kv)
+    allowed = (
+        ((ri >> bits(rows)) == ((ci & (tok - 1)) >> bits(drafts)))
+        & (((ri & (rows - 1)) >> bg) == (ci >> bits(tok)))
+        & ((ci & (drafts - 1)) <= (ri & (drafts - 1)))
+    )
+    ns[...] = jnp.where(allowed, mm_t(qp[...], fresh), NEGATIVE)
+
+    loads[2].wait()
+    ctx = kv.shape[1] // n_kv
+    slot = lax.broadcasted_iota(jnp.int32, (rows, ctx * n_kv), 1)
+    group = lax.broadcasted_iota(jnp.int32, (rows, ctx * n_kv), 0) >> bg
+    same = (slot & (n_kv - 1)) == group
+    for r in range(reqs):
+        cached = kv[r]
+        old = mm_t(qp[r * rows : (r + 1) * rows], cached)
+        old = jnp.where(same & (slot < n_kv * lens_ref[r]), old, NEGATIVE)
+        new = ns[r * rows : (r + 1) * rows]
+        top = jnp.maximum(jnp.max(old, axis=1, keepdims=True), jnp.max(new, axis=1, keepdims=True))
+        old = jnp.exp(old - top)
+        new = jnp.exp(new - top)
+        total = jnp.sum(old, axis=1, keepdims=True) + jnp.sum(new, axis=1, keepdims=True)
+        mixed = mm(old.astype(BF), cached) + mm(new.astype(BF), fresh)
+        oh[r * rows : (r + 1) * rows] = (mixed / total).astype(BF)
+
+    back = mm(permutation(True), oh[...])
+    for b in range(n_heads // 2):
+        first = back[2 * b * tok : (2 * b + 1) * tok]
+        second = back[(2 * b + 1) * tok : (2 * b + 2) * tok]
+        heads[:, b * 128 : (b + 1) * 128] = jnp.where(left, pltpu.roll(first, 64, 1), second).astype(BF)
+
+    loads[3].wait()
+    me = t * ndp + d
+
+    def project(i):
+        b = (d + 1 + i) % ndp
+        part = mm(heads[...], wo[:, pl.ds(pl.multiple_of(b * fb, fb), fb)])
+        p1[b] = (part + 0.5 * whb[b].astype(F32)).astype(BF)
+        return b
+
+    def to_all(i, k):
+        b = project(i)
+        for u in range(2):
+            remote(p1.at[b], mids.at[t, d], a_s.at[u * ndp + b], a_r.at[me], (s, u, b)).start()
+        return k
+
+    lax.fori_loop(0, ndp - 1, to_all, 0)
+    project(ndp - 1)
+    remote(p1.at[d], mids.at[t, d], a_s.at[(1 - t) * ndp + d], a_r.at[me], (s, 1 - t, d)).start()
+    mids[t, d] = p1[d]
+
+    for k in range(1, 2 * ndp):
+        peer = (me + k) % (2 * ndp)
+        pt, pd = peer // ndp, peer % ndp
+        remote(p1.at[pd], mids.at[pt, pd], a_s.at[peer], a_r.at[peer], (s, pt, pd)).wait_recv()
+
+    gain2 = gain2_ref[pl.ds(d, 1), :]
+    for b in range(ndp):
+        m = (mids[0, b].astype(F32) + mids[1, b].astype(F32)).astype(BF)
+        mid[b] = m
+        m = m.astype(F32)
+        sq = m * m
+        row = sq[:, :128]
+        for j in range(1, fb // 128):
+            row = row + sq[:, j * 128 : (j + 1) * 128]
+        sqs[b] = row
+        xs[b % 2, b // 2] = (m * gain2).astype(BF)
+    for k in range(1, ndp):
+        b = (d + k) % ndp
+        remote(sqs.at[b], sqr.at[d], q_s.at[b], q_r.at[d], (s, t, b)).start()
+    sqr[d] = sqs[d]
+
+    loads[4].wait()
+    loads[5].wait()
+    twin = d + 1 - 2 * y
+    theirs = xs[1 - y].reshape(half * tok, fb)
+    for i in range(ff // 512):
+        cols = slice(i * 512, (i + 1) * 512)
+        ups = slice(ff + i * 512, ff + (i + 1) * 512)
+        ybuf[:, :, cols] = mm(theirs, wg[:, cols]).astype(BF).reshape(half, tok, 512)
+        ybuf[:, :, ups] = mm(theirs, wu[:, cols]).astype(BF).reshape(half, tok, 512)
+    order = [(z + k) % half for k in range(1, half + 1)]
+    for zz in order:
+        remote(ybuf.at[zz], yrec.at[zz], y_s.at[zz], y_r.at[zz], (s, t, twin)).start()
+    own = xs[y].reshape(half * tok, fb)
+    for i in range(ff // 512):
+        cols = slice(i * 512, (i + 1) * 512)
+        ups = slice(ff + i * 512, ff + (i + 1) * 512)
+        acc[:, :, cols] = mm(own, wg[:, cols]).reshape(half, tok, 512)
+        acc[:, :, ups] = mm(own, wu[:, cols]).reshape(half, tok, 512)
+    for zz in order[:-1]:
+        remote(ybuf.at[zz], yrec.at[zz], y_s.at[zz], y_r.at[zz], (s, t, twin)).wait_recv()
+        zbuf[zz] = (acc[zz] + yrec[zz].astype(F32)).astype(BF)
+        remote(zbuf.at[zz], zrec.at[z], z_s.at[zz], z_r.at[z], (s, t, zz * 2 + y)).start()
+    remote(ybuf.at[z], yrec.at[z], y_s.at[z], y_r.at[z], (s, t, twin)).wait_recv()
+    for k in range(1, ndp):
+        b = (d + k) % ndp
+        remote(sqs.at[b], sqr.at[b], q_s.at[b], q_r.at[b], (s, t, b)).wait_recv()
+    sums = sqr[0]
+    for b in range(1, ndp):
+        sums = sums + sqr[b]
+    scale = lax.rsqrt(jnp.sum(sums, axis=1, keepdims=True) * (1.0 / width) + EPS)
+    for zz in order[:-1]:
+        remote(zbuf.at[zz], zrec.at[zz], z_s.at[zz], z_r.at[zz], (s, t, zz * 2 + y)).wait_recv()
+    for i in range(ff // 512):
+        pair = []
+        for start in (i * 512, ff + i * 512):
+            cols = slice(start, start + 512)
+            v = acc[z, :, cols] + yrec[z, :, cols].astype(F32)
+            for zz in order[:-1]:
+                v = v + zrec[zz, :, cols].astype(F32)
+            pair.append(v * scale)
+        gate, up = pair
+        acts[y, z, :, i * 512 : (i + 1) * 512] = (gate / (1.0 + jnp.exp(-gate)) * up).astype(BF)
+
+    for zz in order[:-1]:
+        remote(acts.at[y, z], acts.at[y, z], g_s.at[zz], g_r.at[y * half + z], (s, t, zz * 2 + y)).start()
+    remote(acts.at[y, z], acts.at[y, z], h_s.at[z], g_r.at[y * half + z], (s, t, twin)).start()
+    for zz in order[:-1]:
+        remote(acts.at[y, zz], acts.at[y, zz], g_s.at[zz], g_r.at[y * half + zz], (s, t, zz * 2 + y)).wait_recv()
+        remote(acts.at[y, zz], acts.at[y, zz], h_s.at[zz], g_r.at[y * half + zz], (s, t, twin)).start()
+
+    loads[6].wait()
+    home = d // half
+    place = t * half + d % half
+
+    def finish(parity):
+        hidden = acts[parity].reshape(half * tok, ff)
+        grown = mm_t(hidden, wd[...])
+        for zz in range(half):
+            b = zz * 2 + parity
+            value = grown[zz * tok : (zz + 1) * tok] + 0.5 * mid[b].astype(F32)
+            fbuf[b] = value.astype(BF)
+        for zz in order:
+            b = zz * 2 + parity
+            away = (b != d) | (home != t)
+
+            @pl.when(away)
+            def _():
+                remote(fbuf.at[b], fin.at[place], f_s.at[b], f_r.at[place], (s, home, b)).start()
+
+            @pl.when(jnp.logical_not(away))
+            def _():
+                fin[place] = fbuf[b]
+
+    finish(y)
+    for zz in order:
+        remote(acts.at[1 - y, zz], acts.at[1 - y, zz], h_s.at[zz], g_r.at[(1 - y) * half + zz], (s, t, twin)).wait_recv()
+    finish(1 - y)
+
+    for k in range(ndp):
+        src_t, src_d = k // half, t * half + k % half
+        own_block = (src_t == t) & (src_d == d)
+
+        @pl.when(jnp.logical_not(own_block))
+        def _():
+            remote(fbuf.at[0], fin.at[k], f_s.at[0], f_r.at[k], (s, src_t, src_d)).wait_recv()
+
+    for j in range(half):
+        updated = (fin[j].astype(F32) + fin[half + j].astype(F32)).astype(BF).astype(F32)
+        value = jnp.where(keep, updated, whb[t * half + j].astype(F32)).astype(BF)
+        out_ref[:, j * fb : (j + 1) * fb] = value
+        res[:, j * fb : (j + 1) * fb] = value
+
+    @pl.when(s == 0)
+    def _():
+        for k in range(2):
+            remote(res, cur.at[t], c_s.at[k], c_r.at[t], (1, k, d)).start()
+        for k in range(2):
+            remote(res, cur.at[t], c_s.at[k], c_r.at[t], (1, k, d)).wait_send()
+
+    for copy in pending:
+        copy.wait_send()
+    for k in range(1, 2 * ndp):
+        peer = (me + k) % (2 * ndp)
+        pt, pd = peer // ndp, peer % ndp
+        remote(p1.at[pd], mids.at[t, d], a_s.at[peer], a_r.at[peer], (s, pt, pd)).wait_send()
+    for k in range(1, ndp):
+        b = (d + k) % ndp
+        remote(sqs.at[b], sqr.at[d], q_s.at[b], q_r.at[d], (s, t, b)).wait_send()
+    for zz in order:
+        remote(ybuf.at[zz], yrec.at[zz], y_s.at[zz], y_r.at[zz], (s, t, twin)).wait_send()
+        remote(acts.at[y, zz], acts.at[y, zz], h_s.at[zz], g_r.at[y * half + zz], (s, t, twin)).wait_send()
+    for zz in order[:-1]:
+        remote(zbuf.at[zz], zrec.at[z], z_s.at[zz], z_r.at[z], (s, t, zz * 2 + y)).wait_send()
+        remote(acts.at[y, z], acts.at[y, z], g_s.at[zz], g_r.at[y * half + z], (s, t, zz * 2 + y)).wait_send()
+    for b in range(ndp):
+
+        @pl.when((b != d) | (home != t))
+        def _():
+            remote(fbuf.at[b], fin.at[place], f_s.at[b], f_r.at[place], (s, home, b)).wait_send()
+
+
+def fused(
+    exit_hidden,
+    exit_depth,
+    context_len,
+    attn_gain,
+    w_query,
+    w_keyval,
+    w_out,
+    kv_cache,
+    mlp_gain,
+    w_gate,
+    w_up,
+    w_down,
+):
+    ndp = lax.axis_size("dp")
+    reqs, drafts, piece = exit_hidden.shape
+    tok = reqs * drafts
+    width = w_query.shape[1]
+    fb = width // ndp
+    half = ndp // 2
+    ff = w_gate.shape[2]
+    n_kv = kv_cache.shape[3]
+    ctx = kv_cache.shape[2]
+    q_cols = w_query.shape[2]
+    n_heads = q_cols // 64
+    places = jnp.repeat(context_len, drafts) + jnp.tile(jnp.arange(drafts, dtype=jnp.int32), reqs)
+    lane = jnp.arange(128, dtype=jnp.int32)
+    rates = jnp.exp((lane % 32).astype(F32) * (-2.0 * math.log(THETA) / 64))
+    angles = places.astype(F32)[:, None] * rates
+    cosine = jnp.cos(angles)
+    sine = jnp.where((lane & 63) < 32, -1.0, 1.0) * jnp.sin(angles)
+    depth = jnp.broadcast_to(jnp.repeat(exit_depth, drafts)[:, None], (tok, 128))
+    hbm = pl.BlockSpec(memory_space=pl.ANY)
+    vmem = pl.BlockSpec(memory_space=pltpu.VMEM)
+    smem = pl.BlockSpec(memory_space=pltpu.SMEM)
+    dma = pltpu.SemaphoreType.DMA
+    V = pltpu.VMEM
+    out = pl.pallas_call(
+        functools.partial(fused_kernel, ndp),
+        out_shape=jax.ShapeDtypeStruct((tok, width // 2), BF),
+        in_specs=[smem, vmem, vmem, vmem, vmem, vmem, vmem] + [hbm] * 7,
+        out_specs=vmem,
+        scratch_shapes=[
+            V(w_query.shape[1:], BF),
+            V(w_keyval.shape[1:], BF),
+            V((reqs, ctx * n_kv, 128), BF),
+            V(w_out.shape[1:], BF),
+            V(w_gate.shape[1:], BF),
+            V(w_up.shape[1:], BF),
+            V(w_down.shape[1:], BF),
+            V((4, tok, piece), BF),
+            V((2, tok, width // 2), BF),
+            V((ndp, tok, fb), BF),
+            V((tok, q_cols), F32),
+            V((tok, n_kv * 128), F32),
+            V((n_heads * tok, 128), BF),
+            V((n_heads * tok, n_kv * tok), F32),
+            V((n_heads * tok, 128), BF),
+            V((tok, q_cols), BF),
+            V((ndp, tok, fb), BF),
+            V((2, ndp, tok, fb), BF),
+            V((ndp, tok, fb), BF),
+            V((2, half, tok, fb), BF),
+            V((ndp, tok, 128), F32),
+            V((ndp, tok, 128), F32),
+            V((half, tok, 2 * ff), BF),
+            V((half, tok, 2 * ff), BF),
+            V((half, tok, 2 * ff), F32),
+            V((half, tok, 2 * ff), BF),
+            V((half, tok, 2 * ff), BF),
+            V((2, half, tok, ff), BF),
+            V((ndp, tok, fb), BF),
+            V((ndp, tok, fb), BF),
+            V((tok, width // 2), BF),
+            dma((7,)),
+            dma((3,)), dma((4,)),
+            dma((2 * ndp,)), dma((2 * ndp,)),
+            dma((ndp,)), dma((ndp,)),
+            dma((half,)), dma((half,)),
+            dma((half,)), dma((half,)),
+            dma((half,)), dma((ndp,)), dma((half,)),
+            dma((ndp,)), dma((ndp,)),
+            dma((2,)), dma((2,)),
+        ],
+        compiler_params=pltpu.CompilerParams(
+            collective_id=0, has_side_effects=True, vmem_limit_bytes=60 * 1024 * 1024
+        ),
+    )(
+        context_len,
+        depth,
+        cosine,
+        sine,
+        attn_gain,
+        mlp_gain.reshape(ndp, fb),
+        exit_hidden.reshape(tok, piece),
+        w_query[0],
+        w_keyval[0],
+        kv_cache.reshape(reqs, ctx * n_kv, 128),
+        w_out[0],
+        w_gate[0],
+        w_up[0],
+        w_down[0],
+    )
+    return out.reshape(1, reqs, drafts, width // 2)
+
+
 def solution(mesh):
     in_specs = (
         P("dp", None, ("section", "tensor")),
@@ -209,4 +674,13 @@
         P("section", "dp", "tensor"),
     )
     out_specs = P("section", "dp", None, "tensor")
-    return jax.shard_map(local, mesh=mesh, in_specs=in_specs, out_specs=out_specs, check_vma=False)
+    count = mesh.shape["dp"]
+    fits = (
+        mesh.shape["section"] == 2
+        and mesh.shape["tensor"] == 2
+        and count & (count - 1) == 0
+        and count >= 4
+        and (D // count) % 128 == 0
+    )
+    body = fused if fits else local
+    return jax.shard_map(body, mesh=mesh, in_specs=in_specs, out_specs=out_specs, check_vma=False)

time: 563 us -> 122 us (0.22)
  waiting for transfers between devices: 475 us -> 0 us
  Pallas kernels: 0 us -> 113 us
  matrix products: 27 us -> 0 us
  between operations: 13.5 us -> 0.02 us
  local copies, waits for them, and re-layouts: 18.9 us -> 5.56 us
  blocking collectives: 10.2 us -> 0 us
  other arithmetic: 10.5 us -> 2.85 us
    all_gather x3 -> x0, waiting for transfers between devices: 351 us -> none  [the longest x1 125 us: local(): lax.all_gather(w_down[0], 'dp', axis=0, tiled=True)]
    psum x4 -> x0, waiting for transfers between devices: 118 us -> none  [the longest x2 61.9 us: turn_step(): summed = lax.psum(partial_value, 'tensor').reshape(members, DRAFT, D)]
    pallas_call x0 -> x1, Pallas kernels: none -> 113 us  [fused(): pl.pallas_call(functools.partial(fused_kernel, ndp), out_shape=jax.ShapeD...]
    dot_general x9 -> x0, matrix products: 27 us -> none  [the longest x1 9.81 us: feed_forward(): lax.dot_general(act, down_full, (((1,), (1,)), ((), ())), preferred_eleme...]
    all_gather x1 -> x0, blocking collectives: 10.2 us -> none  [local(): lax.all_gather(exit_hidden, ('section', 'tensor'), axis=2, tiled=True)]
    unnamed x14 -> x1, local copies, waits for them, and re-layouts: 10.4 us -> 0.51 us
  transfers between devices with their start and end apart: 9 -> 0, of which waited for: 9 -> 0; matrix products, arithmetic and copies ran while one was open for 3% -> 0% of each run, Pallas kernels for 0% -> 0%
where the time goes in v1:
time: 122 us
  Pallas kernels  113 us (93%)
  local copies, waits for them, and re-layouts  5.56 us (5%)
  other arithmetic  2.85 us (2%)
    pallas_call x1, Pallas kernels, fused(): pl.pallas_call(functools.partial(fused_kernel, ndp), out_shape=jax.ShapeD...  113 us

profile of v1, /device:TPU:3, one launch (start us, length us, event | category | flops | bytes accessed | tf_op | source)
XLA Modules:
  0.0 121.7 jit_solution(12484674406348165171)
XLA Ops:
  0.0 0.7 broadcast_in_dim.24
  0.7 0.1 broadcast_in_dim.25
  0.8 0.7 add_convert_fusion
  1.5 0.1 convert_element_type.18
  1.6 0.5 broadcast.44
  2.1 1.4 %reduce.3 = f32[2048]{0:T(1024)S(1)} reduce(f32[1,2048]{1,0:T(1,128)} %param.20, f32[]{:T(128)} %broadcast.44), dimensions={0}, to_apply=%param.20.reduce_sub_computation.3 | reduce | bytes 16388 | tf_op args[8]
  3.5 0.6 reshape.44.gain2_ref
  4.1 0.7 broadcast_in_dim.26.depth_ref
  4.8 0.7 fusion
  5.5 1.4 %reshape.45.entry_ref = bf16[32,512]{1,0:T(8,128)(2,1)} reshape(bf16[8,4,512]{2,1,0:T(4,128)(2,1)} %param.12) | data formatting | bytes 65536 | tf_op jit(solution)/shard_map/reshape | solution.py:649
  6.9 113.3 %shard_map.118 = bf16[32,1024]{1,0:T(8,128)(2,1)} custom-call(s32[8]{0:T(128)} %lens_ref.1, s32[32,128]{1,0:T(8,128)} %broadcast_in_dim.26.depth_ref, f32[32,128]{1,0:T(8,128)} %get-tuple-element.6.cos_ref, f32[32,128]{1,0:T(8,128)} %get-tuple-element.5.sin_ref, f32[1,2048]{1,0:T(1,128)} %gain_ref.1, f32[8,256]{1,0:T(8,128)} %reshape.44.gain2_ref, ...), custom_call_target="tpu_custom_call" | custom-call | tf_op jit(solution)/shard_map/pallas_call | solution.py:592
  120.2 1.5 %reshape.47 = bf16[1,8,4,1024]{3,2,1,0:T(4,128)(2,1)} reshape(bf16[32,1024]{1,0:T(8,128)(2,1)} %shard_map.118) | data formatting | bytes 131072 | tf_op jit(solution)/shard_map/reshape | solution.py:658
  (1 shorter events, 0.0 us)

commit v2 on v1

--- a/solution.py
+++ b/solution.py
@@ -198,6 +198,7 @@
 
 
 MESH = pl.DeviceIdType.MESH
+CHUNKS = 2
 BF = jnp.bfloat16
 F32 = jnp.float32
 
@@ -222,8 +223,6 @@
     ndp,
     lens_ref,
     depth_ref,
-    cos_ref,
-    sin_ref,
     gain_ref,
     gain2_ref,
     entry_ref,
@@ -236,11 +235,11 @@
     wd_hbm,
     out_ref,
     wq, wkv, kv, wo, wg, wu, wd,
-    ent, cur, whb, qs, kvs, qp, ns, oh, heads,
+    ent, ew, cur, perms, whb, qs, kvs, qp, ns, oh, heads,
     p1, mids, mid, xs, sqs, sqr,
-    ybuf, yrec, acc, zbuf, zrec, acts, fbuf, fin, res,
-    ld_sem, ent_s, ent_r, a_s, a_r, q_s, q_r, y_s, y_r, z_s, z_r,
-    g_s, g_r, h_s, f_s, f_r, c_s, c_r,
+    zbuf, zrec, acts, fbuf, fin, res,
+    ld_sem, w_s, w_r, go, ent_s, ent_r, a_s, a_r, q_s, q_r, z_s, z_r,
+    g_s, g_r, f_s, f_r, c_s, c_r,
 ):
     s = lax.axis_index("section")
     t = lax.axis_index("tensor")
@@ -248,36 +247,53 @@
     half = ndp // 2
     z = d // 2
     y = d % 2
-    tok, width = cos_ref.shape[0], gain_ref.shape[1]
-    fb = width // ndp
-    reqs = lens_ref.shape[0]
-    drafts = tok // reqs
+    twin = d + 1 - 2 * y
+    reqs, drafts, piece = entry_ref.shape
+    tok = reqs * drafts
+    width = gain_ref.shape[1]
+    fb = width // half
     n_heads = wq.shape[1] // 64
     n_kv = wkv.shape[1] // 128
-    ff = wg.shape[1]
+    ff = wg.shape[2]
+    chunks, cw = acts.shape[0], acts.shape[3]
     rows = n_heads * drafts
 
     loads = [
         pltpu.make_async_copy(src, dst, ld_sem.at[i])
         for i, (src, dst) in enumerate(
-            [(wq_hbm, wq), (wkv_hbm, wkv), (kv_hbm, kv), (wo_hbm, wo), (wg_hbm, wg), (wu_hbm, wu), (wd_hbm, wd)]
+            [
+                (wq_hbm, wq),
+                (wkv_hbm, wkv),
+                (kv_hbm, kv),
+                (wo_hbm, wo),
+                (wg_hbm, wg.at[y]),
+                (wu_hbm, wu.at[y]),
+                (wd_hbm, wd.at[y]),
+            ]
         )
     ]
     for one in loads:
         one.start()
 
     barrier = pltpu.get_barrier_semaphore()
-    for k in range(1, 2 * ndp):
-        peer = (t * ndp + d + k) % (2 * ndp)
-        pl.semaphore_signal(barrier, inc=1, device_id=(s, peer // ndp, peer % ndp), device_id_type=MESH)
+    lane_me = t * half + z
+    for k in range(1, 2 * half):
+        peer = (lane_me + k) % (2 * half)
+        where = (s, peer // half, peer % half * 2 + y)
+        pl.semaphore_signal(barrier, inc=1, device_id=where, device_id_type=MESH)
     for k in range(2):
         pl.semaphore_signal(barrier, inc=1, device_id=(1 - s, k, d), device_id_type=MESH)
-    pl.semaphore_wait(barrier, 2 * ndp + 1)
+    pl.semaphore_signal(barrier, inc=1, device_id=(s, t, twin), device_id_type=MESH)
+    pl.semaphore_wait(barrier, 2 * half + 2)
 
     def remote(src, dst, send, recv, where):
         return pltpu.make_async_remote_copy(
             src_ref=src, dst_ref=dst, send_sem=send, recv_sem=recv, device_id=where, device_id_type=MESH
         )
+
+    def twin_copy(k):
+        src, dst = [(wg_hbm, wg), (wu_hbm, wu), (wd_hbm, wd)][k]
+        return remote(src, dst.at[y], w_s.at[k], w_r.at[k], (s, t, twin))
 
     mine = s * 2 + t
     pending = []
@@ -288,6 +304,11 @@
         pending.append(copy)
     ent[mine] = entry_ref[...]
 
+    @pl.when(s == 0)
+    def _():
+        for k in range(3):
+            twin_copy(k).start()
+
     def permutation(transposed):
         i = lax.broadcasted_iota(jnp.int32, (n_heads * tok,) * 2, 1 if transposed else 0)
         c = lax.broadcasted_iota(jnp.int32, (n_heads * tok,) * 2, 0 if transposed else 1)
@@ -295,28 +316,50 @@
         target = ((i & (rows - 1)) >> bd << bt) + (i >> br << bd) + (i & (drafts - 1))
         return jnp.where(target == c, 1.0, 0.0).astype(BF)
 
+    perms[0] = permutation(False)
+    perms[1] = permutation(True)
+    row = lax.broadcasted_iota(jnp.int32, (tok, 128), 0)
+    lane = lanes_like((tok, 128))
+    low = (lane & 63) < 32
+    left = lane < 64
+    length = jnp.zeros((tok, 128), jnp.int32)
+    depth = jnp.zeros((tok, 128), jnp.int32)
+    for r in range(reqs):
+        here = (row >> bits(drafts)) == r
+        length = jnp.where(here, lens_ref[r], length)
+        depth = jnp.where(here, depth_ref[r], depth)
+    rates = jnp.exp((lane & 31).astype(F32) * (-2.0 * math.log(THETA) / 64))
+    angles = (length + (row & (drafts - 1))).astype(F32) * rates
+    cosine = jnp.cos(angles)
+    sine = jnp.where(low, -1.0, 1.0) * jnp.sin(angles)
+    take = depth[:, :1] >= s
+    keep = depth[:, :1] <= s
+
     for k in range(1, 4):
         other = (mine + k) % 4
         remote(entry_ref, ent.at[other], ent_s.at[k - 1], ent_r.at[other], (other // 2, other % 2, d)).wait_recv()
 
+    for q in range(4):
+        for r in range(reqs):
+            ew[r * drafts : (r + 1) * drafts, q * piece : (q + 1) * piece] = ent[q, r].astype(F32)
+
     @pl.when(s == 0)
     def _():
         cur[...] = jnp.zeros_like(cur)
 
     @pl.when(s == 1)
     def _():
+        pl.semaphore_wait(go, 1)
+        for k in range(3):
+            twin_copy(k).start()
         for k in range(2):
             remote(res, cur.at[k], c_s.at[k], c_r.at[k], (0, k, d)).wait_recv()
 
-    depth = depth_ref[...][:, :1]
-    take = depth >= s
-    keep = depth <= s
     wide = []
     total_sq = None
-    per_ent = ent.shape[2] // fb
     per_cur = cur.shape[2] // fb
-    for b in range(ndp):
-        e = ent[b // per_ent, :, (b % per_ent) * fb : (b % per_ent + 1) * fb].astype(F32)
+    for b in range(half):
+        e = ew[:, b * fb : (b + 1) * fb]
         c = cur[b // per_cur, :, (b % per_cur) * fb : (b % per_cur + 1) * fb].astype(F32)
         w = jnp.where(take, e, c)
         whb[b] = w.astype(BF)
@@ -335,12 +378,6 @@
     for i in range(wkv.shape[1] // 256):
         kvs[:, i * 256 : (i + 1) * 256] = mm(normed, wkv[:, i * 256 : (i + 1) * 256])
 
-    cosine = cos_ref[...]
-    sine = sin_ref[...]
-    lane = lanes_like((tok, 128))
-    low = (lane & 63) < 32
-    left = lane < 64
-
     def turned(x):
         partner = jnp.where(low, pltpu.roll(x, 96, 1), pltpu.roll(x, 32, 1))
         return x * cosine + partner * sine
@@ -350,7 +387,7 @@
         x = turned(qs[:, b * 128 : (b + 1) * 128]) * (64 ** -0.5)
         stacked.append(jnp.where(left, x, 0.0).astype(BF))
         stacked.append(jnp.where(left, pltpu.roll(x, 64, 1), 0.0).astype(BF))
-    qp[...] = mm(permutation(False), jnp.concatenate(stacked, axis=0)).astype(BF)
+    qp[...] = mm(perms[0], jnp.concatenate(stacked, axis=0)).astype(BF)
     fresh = []
     for h in range(n_kv):
         x = kvs[:, h * 128 : (h + 1) * 128]
@@ -384,17 +421,16 @@
         mixed = mm(old.astype(BF), cached) + mm(new.astype(BF), fresh)
         oh[r * rows : (r + 1) * rows] = (mixed / total).astype(BF)
 
-    back = mm(permutation(True), oh[...])
+    back = mm(perms[1], oh[...])
     for b in range(n_heads // 2):
         first = back[2 * b * tok : (2 * b + 1) * tok]
         second = back[(2 * b + 1) * tok : (2 * b + 2) * tok]
         heads[:, b * 128 : (b + 1) * 128] = jnp.where(left, pltpu.roll(first, 64, 1), second).astype(BF)
 
     loads[3].wait()
-    me = t * ndp + d
 
     def project(i):
-        b = (d + 1 + i) % ndp
+        b = (z + 1 + i) % half
         part = mm(heads[...], wo[:, pl.ds(pl.multiple_of(b * fb, fb), fb)])
         p1[b] = (part + 0.5 * whb[b].astype(F32)).astype(BF)
         return b
@@ -402,154 +438,144 @@
     def to_all(i, k):
         b = project(i)
         for u in range(2):
-            remote(p1.at[b], mids.at[t, d], a_s.at[u * ndp + b], a_r.at[me], (s, u, b)).start()
+            remote(p1.at[b], mids.at[t, z], a_s.at[u, b], a_r.at[t, z], (s, u, b * 2 + y)).start()
         return k
 
-    lax.fori_loop(0, ndp - 1, to_all, 0)
-    project(ndp - 1)
-    remote(p1.at[d], mids.at[t, d], a_s.at[(1 - t) * ndp + d], a_r.at[me], (s, 1 - t, d)).start()
-    mids[t, d] = p1[d]
-
-    for k in range(1, 2 * ndp):
-        peer = (me + k) % (2 * ndp)
-        pt, pd = peer // ndp, peer % ndp
-        remote(p1.at[pd], mids.at[pt, pd], a_s.at[peer], a_r.at[peer], (s, pt, pd)).wait_recv()
-
-    gain2 = gain2_ref[pl.ds(d, 1), :]
-    for b in range(ndp):
+    lax.fori_loop(0, half - 1, to_all, 0)
+    project(half - 1)
+    remote(p1.at[z], mids.at[t, z], a_s.at[1 - t, z], a_r.at[t, z], (s, 1 - t, d)).start()
+    mids[t, z] = p1[z]
+
+    others = []
+    for k in range(1, 2 * half):
+        peer = (lane_me + k) % (2 * half)
+        others.append((peer // half, peer % half))
+    for pt, pz in others:
+        remote(p1.at[pz], mids.at[pt, pz], a_s.at[pt, pz], a_r.at[pt, pz], (s, pt, pz * 2 + y)).wait_recv()
+
+    gain2 = gain2_ref[:, pl.ds(pl.multiple_of(z * fb, fb), fb)]
+    for b in range(half):
         m = (mids[0, b].astype(F32) + mids[1, b].astype(F32)).astype(BF)
         mid[b] = m
         m = m.astype(F32)
         sq = m * m
-        row = sq[:, :128]
+        part = sq[:, :128]
         for j in range(1, fb // 128):
-            row = row + sq[:, j * 128 : (j + 1) * 128]
-        sqs[b] = row
-        xs[b % 2, b // 2] = (m * gain2).astype(BF)
-    for k in range(1, ndp):
-        b = (d + k) % ndp
-        remote(sqs.at[b], sqr.at[d], q_s.at[b], q_r.at[d], (s, t, b)).start()
-    sqr[d] = sqs[d]
+            part = part + sq[:, j * 128 : (j + 1) * 128]
+        sqs[b] = part
+        xs[b] = (m * gain2).astype(BF)
+    order = [(z + k) % half for k in range(1, half)]
+    for zz in order:
+        remote(sqs.at[zz], sqr.at[z], q_s.at[zz], q_r.at[z], (s, t, zz * 2 + y)).start()
+    sqr[z] = sqs[z]
 
     loads[4].wait()
     loads[5].wait()
-    twin = d + 1 - 2 * y
-    theirs = xs[1 - y].reshape(half * tok, fb)
-    for i in range(ff // 512):
-        cols = slice(i * 512, (i + 1) * 512)
-        ups = slice(ff + i * 512, ff + (i + 1) * 512)
-        ybuf[:, :, cols] = mm(theirs, wg[:, cols]).astype(BF).reshape(half, tok, 512)
-        ybuf[:, :, ups] = mm(theirs, wu[:, cols]).astype(BF).reshape(half, tok, 512)
-    order = [(z + k) % half for k in range(1, half + 1)]
+    for k in range(2):
+        twin_copy(k).wait()
+
+    @pl.when(s == 0)
+    def _():
+        pl.semaphore_signal(go, inc=1, device_id=(1, t, d), device_id_type=MESH)
+
+    grid = xs[...].reshape(half * tok, fb)
+    step = 512
+    for c in range(chunks):
+        for i in range(cw // step):
+            src = slice(c * cw + i * step, c * cw + (i + 1) * step)
+            for g, w in enumerate((wg, wu)):
+                dst = slice(g * cw + i * step, g * cw + (i + 1) * step)
+                zbuf[c, :, :, dst] = mm(grid, w[:, :, src].reshape(fb, step)).astype(BF).reshape(half, tok, step)
+        for zz in order:
+            remote(zbuf.at[c, zz], zrec.at[c, z], z_s.at[c, zz], z_r.at[c, z], (s, t, zz * 2 + y)).start()
+
     for zz in order:
-        remote(ybuf.at[zz], yrec.at[zz], y_s.at[zz], y_r.at[zz], (s, t, twin)).start()
-    own = xs[y].reshape(half * tok, fb)
-    for i in range(ff // 512):
-        cols = slice(i * 512, (i + 1) * 512)
-        ups = slice(ff + i * 512, ff + (i + 1) * 512)
-        acc[:, :, cols] = mm(own, wg[:, cols]).reshape(half, tok, 512)
-        acc[:, :, ups] = mm(own, wu[:, cols]).reshape(half, tok, 512)
-    for zz in order[:-1]:
-        remote(ybuf.at[zz], yrec.at[zz], y_s.at[zz], y_r.at[zz], (s, t, twin)).wait_recv()
-        zbuf[zz] = (acc[zz] + yrec[zz].astype(F32)).astype(BF)
-        remote(zbuf.at[zz], zrec.at[z], z_s.at[zz], z_r.at[z], (s, t, zz * 2 + y)).start()
-    remote(ybuf.at[z], yrec.at[z], y_s.at[z], y_r.at[z], (s, t, twin)).wait_recv()
-    for k in range(1, ndp):
-        b = (d + k) % ndp
-        remote(sqs.at[b], sqr.at[b], q_s.at[b], q_r.at[b], (s, t, b)).wait_recv()
+        remote(sqs.at[zz], sqr.at[zz], q_s.at[zz], q_r.at[zz], (s, t, zz * 2 + y)).wait_recv()
     sums = sqr[0]
-    for b in range(1, ndp):
+    for b in range(1, half):
         sums = sums + sqr[b]
     scale = lax.rsqrt(jnp.sum(sums, axis=1, keepdims=True) * (1.0 / width) + EPS)
-    for zz in order[:-1]:
-        remote(zbuf.at[zz], zrec.at[zz], z_s.at[zz], z_r.at[zz], (s, t, zz * 2 + y)).wait_recv()
-    for i in range(ff // 512):
-        pair = []
-        for start in (i * 512, ff + i * 512):
-            cols = slice(start, start + 512)
-            v = acc[z, :, cols] + yrec[z, :, cols].astype(F32)
-            for zz in order[:-1]:
-                v = v + zrec[zz, :, cols].astype(F32)
-            pair.append(v * scale)
-        gate, up = pair
-        acts[y, z, :, i * 512 : (i + 1) * 512] = (gate / (1.0 + jnp.exp(-gate)) * up).astype(BF)
-
-    for zz in order[:-1]:
-        remote(acts.at[y, z], acts.at[y, z], g_s.at[zz], g_r.at[y * half + z], (s, t, zz * 2 + y)).start()
-    remote(acts.at[y, z], acts.at[y, z], h_s.at[z], g_r.at[y * half + z], (s, t, twin)).start()
-    for zz in order[:-1]:
-        remote(acts.at[y, zz], acts.at[y, zz], g_s.at[zz], g_r.at[y * half + zz], (s, t, zz * 2 + y)).wait_recv()
-        remote(acts.at[y, zz], acts.at[y, zz], h_s.at[zz], g_r.at[y * half + zz], (s, t, twin)).start()
+    for c in range(chunks):
+        for zz in order:
+            remote(zbuf.at[c, zz], zrec.at[c, zz], z_s.at[c, zz], z_r.at[c, zz], (s, t, zz * 2 + y)).wait_recv()
+        for i in range(cw // step):
+            pair = []
+            for start in (i * step, cw + i * step):
+                cols = slice(start, start + step)
+                v = zbuf[c, z, :, cols].astype(F32)
+                for zz in order:
+                    v = v + zrec[c, zz, :, cols].astype(F32)
+                pair.append(v * scale)
+            gate, up = pair
+            acts[c, z, :, i * step : (i + 1) * step] = (gate / (1.0 + jnp.exp(-gate)) * up).astype(BF)
+        for zz in order:
+            remote(acts.at[c, z], acts.at[c, z], g_s.at[c, zz], g_r.at[c, z], (s, t, zz * 2 + y)).start()
 
     loads[6].wait()
-    home = d // half
-    place = t * half + d % half
-
-    def finish(parity):
-        hidden = acts[parity].reshape(half * tok, ff)
-        grown = mm_t(hidden, wd[...])
-        for zz in range(half):
-            b = zz * 2 + parity
-            value = grown[zz * tok : (zz + 1) * tok] + 0.5 * mid[b].astype(F32)
-            fbuf[b] = value.astype(BF)
+    twin_copy(2).wait()
+    grown = None
+    for c in range(chunks):
         for zz in order:
-            b = zz * 2 + parity
-            away = (b != d) | (home != t)
-
-            @pl.when(away)
-            def _():
-                remote(fbuf.at[b], fin.at[place], f_s.at[b], f_r.at[place], (s, home, b)).start()
-
-            @pl.when(jnp.logical_not(away))
-            def _():
-                fin[place] = fbuf[b]
-
-    finish(y)
+            remote(acts.at[c, zz], acts.at[c, zz], g_s.at[c, zz], g_r.at[c, zz], (s, t, zz * 2 + y)).wait_recv()
+        part = mm_t(acts[c].reshape(half * tok, cw), wd[:, :, c * cw : (c + 1) * cw].reshape(fb, cw))
+        grown = part if grown is None else grown + part
+
+    per_home = half // 2
+    home = z // per_home
+    place = t * per_home + z % per_home
+    for b in range(half):
+        fbuf[b] = (grown[b * tok : (b + 1) * tok] + 0.5 * mid[b].astype(F32)).astype(BF)
     for zz in order:
-        remote(acts.at[1 - y, zz], acts.at[1 - y, zz], h_s.at[zz], g_r.at[(1 - y) * half + zz], (s, t, twin)).wait_recv()
-    finish(1 - y)
-
-    for k in range(ndp):
-        src_t, src_d = k // half, t * half + k % half
-        own_block = (src_t == t) & (src_d == d)
-
-        @pl.when(jnp.logical_not(own_block))
+        remote(fbuf.at[zz], fin.at[place], f_s.at[zz], f_r.at[place], (s, home, zz * 2 + y)).start()
+
+    @pl.when(home != t)
+    def _():
+        remote(fbuf.at[z], fin.at[place], f_s.at[z], f_r.at[place], (s, home, d)).start()
+
+    @pl.when(home == t)
+    def _():
+        fin[place] = fbuf[z]
+
+    for k in range(half):
+        src_t, src_z = k // per_home, t * per_home + k % per_home
+
+        @pl.when(jnp.logical_not((src_t == t) & (src_z == z)))
         def _():
-            remote(fbuf.at[0], fin.at[k], f_s.at[0], f_r.at[k], (s, src_t, src_d)).wait_recv()
-
-    for j in range(half):
-        updated = (fin[j].astype(F32) + fin[half + j].astype(F32)).astype(BF).astype(F32)
-        value = jnp.where(keep, updated, whb[t * half + j].astype(F32)).astype(BF)
-        out_ref[:, j * fb : (j + 1) * fb] = value
-        res[:, j * fb : (j + 1) * fb] = value
+            remote(fbuf.at[0], fin.at[k], f_s.at[0], f_r.at[k], (s, src_t, src_z * 2 + y)).wait_recv()
+
+    for j in range(per_home):
+        updated = (fin[j].astype(F32) + fin[per_home + j].astype(F32)).astype(BF).astype(F32)
+        value = jnp.where(keep, updated, whb[t * per_home + j].astype(F32))
+        res[:, j * fb : (j + 1) * fb] = value.astype(BF)
+        ew[:, j * fb : (j + 1) * fb] = value
 
     @pl.when(s == 0)
     def _():
         for k in range(2):
             remote(res, cur.at[t], c_s.at[k], c_r.at[t], (1, k, d)).start()
+
+    for r in range(reqs):
+        out_ref[r] = ew[r * drafts : (r + 1) * drafts, : width // 2].astype(BF)
+
+    @pl.when(s == 0)
+    def _():
         for k in range(2):
             remote(res, cur.at[t], c_s.at[k], c_r.at[t], (1, k, d)).wait_send()
 
     for copy in pending:
         copy.wait_send()
-    for k in range(1, 2 * ndp):
-        peer = (me + k) % (2 * ndp)
-        pt, pd = peer // ndp, peer % ndp
-        remote(p1.at[pd], mids.at[t, d], a_s.at[peer], a_r.at[peer], (s, pt, pd)).wait_send()
-    for k in range(1, ndp):
-        b = (d + k) % ndp
-        remote(sqs.at[b], sqr.at[d], q_s.at[b], q_r.at[d], (s, t, b)).wait_send()
+    for pt, pz in others:
+        remote(p1.at[pz], mids.at[t, z], a_s.at[pt, pz], a_r.at[pt, pz], (s, pt, pz * 2 + y)).wait_send()
     for zz in order:
-        remote(ybuf.at[zz], yrec.at[zz], y_s.at[zz], y_r.at[zz], (s, t, twin)).wait_send()
-        remote(acts.at[y, zz], acts.at[y, zz], h_s.at[zz], g_r.at[y * half + zz], (s, t, twin)).wait_send()
-    for zz in order[:-1]:
-        remote(zbuf.at[zz], zrec.at[z], z_s.at[zz], z_r.at[z], (s, t, zz * 2 + y)).wait_send()
-        remote(acts.at[y, z], acts.at[y, z], g_s.at[zz], g_r.at[y * half + z], (s, t, zz * 2 + y)).wait_send()
-    for b in range(ndp):
-
-        @pl.when((b != d) | (home != t))
-        def _():
-            remote(fbuf.at[b], fin.at[place], f_s.at[b], f_r.at[place], (s, home, b)).wait_send()
+        remote(sqs.at[zz], sqr.at[z], q_s.at[zz], q_r.at[z], (s, t, zz * 2 + y)).wait_send()
+        for c in range(chunks):
+            remote(zbuf.at[c, zz], zrec.at[c, z], z_s.at[c, zz], z_r.at[c, z], (s, t, zz * 2 + y)).wait_send()
+            remote(acts.at[c, z], acts.at[c, z], g_s.at[c, zz], g_r.at[c, z], (s, t, zz * 2 + y)).wait_send()
+        remote(fbuf.at[zz], fin.at[place], f_s.at[zz], f_r.at[place], (s, home, zz * 2 + y)).wait_send()
+
+    @pl.when(home != t)
+    def _():
+        remote(fbuf.at[z], fin.at[place], f_s.at[z], f_r.at[place], (s, home, d)).wait_send()
 
 
 def fused(
@@ -570,20 +596,15 @@
     reqs, drafts, piece = exit_hidden.shape
     tok = reqs * drafts
     width = w_query.shape[1]
-    fb = width // ndp
     half = ndp // 2
+    fb = width // half
     ff = w_gate.shape[2]
     n_kv = kv_cache.shape[3]
     ctx = kv_cache.shape[2]
     q_cols = w_query.shape[2]
     n_heads = q_cols // 64
-    places = jnp.repeat(context_len, drafts) + jnp.tile(jnp.arange(drafts, dtype=jnp.int32), reqs)
-    lane = jnp.arange(128, dtype=jnp.int32)
-    rates = jnp.exp((lane % 32).astype(F32) * (-2.0 * math.log(THETA) / 64))
-    angles = places.astype(F32)[:, None] * rates
-    cosine = jnp.cos(angles)
-    sine = jnp.where((lane & 63) < 32, -1.0, 1.0) * jnp.sin(angles)
-    depth = jnp.broadcast_to(jnp.repeat(exit_depth, drafts)[:, None], (tok, 128))
+    chunks = CHUNKS
+    cw = ff // chunks
     hbm = pl.BlockSpec(memory_space=pl.ANY)
     vmem = pl.BlockSpec(memory_space=pltpu.VMEM)
     smem = pl.BlockSpec(memory_space=pltpu.SMEM)
@@ -591,49 +612,48 @@
     V = pltpu.VMEM
     out = pl.pallas_call(
         functools.partial(fused_kernel, ndp),
-        out_shape=jax.ShapeDtypeStruct((tok, width // 2), BF),
-        in_specs=[smem, vmem, vmem, vmem, vmem, vmem, vmem] + [hbm] * 7,
+        out_shape=jax.ShapeDtypeStruct((reqs, drafts, width // 2), BF),
+        in_specs=[smem, smem, vmem, vmem, vmem] + [hbm] * 7,
         out_specs=vmem,
         scratch_shapes=[
             V(w_query.shape[1:], BF),
             V(w_keyval.shape[1:], BF),
             V((reqs, ctx * n_kv, 128), BF),
             V(w_out.shape[1:], BF),
-            V(w_gate.shape[1:], BF),
-            V(w_up.shape[1:], BF),
-            V(w_down.shape[1:], BF),
-            V((4, tok, piece), BF),
+            V((2, fb // 2, ff), BF),
+            V((2, fb // 2, ff), BF),
+            V((2, fb // 2, ff), BF),
+            V((4, reqs, drafts, piece), BF),
+            V((tok, width), F32),
             V((2, tok, width // 2), BF),
-            V((ndp, tok, fb), BF),
+            V((2, n_heads * tok, n_heads * tok), BF),
+            V((half, tok, fb), BF),
             V((tok, q_cols), F32),
             V((tok, n_kv * 128), F32),
             V((n_heads * tok, 128), BF),
             V((n_heads * tok, n_kv * tok), F32),
             V((n_heads * tok, 128), BF),
             V((tok, q_cols), BF),
-            V((ndp, tok, fb), BF),
-            V((2, ndp, tok, fb), BF),
-            V((ndp, tok, fb), BF),
+            V((half, tok, fb), BF),
             V((2, half, tok, fb), BF),
-            V((ndp, tok, 128), F32),
-            V((ndp, tok, 128), F32),
-            V((half, tok, 2 * ff), BF),
-            V((half, tok, 2 * ff), BF),
-            V((half, tok, 2 * ff), F32),
-            V((half, tok, 2 * ff), BF),
-            V((half, tok, 2 * ff), BF),
-            V((2, half, tok, ff), BF),
-            V((ndp, tok, fb), BF),
-            V((ndp, tok, fb), BF),
+            V((half, tok, fb), BF),
+            V((half, tok, fb), BF),
+            V((half, tok, 128), F32),
+            V((half, tok, 128), F32),
+            V((chunks, half, tok, 2 * cw), BF),
+            V((chunks, half, tok, 2 * cw), BF),
+            V((chunks, half, tok, cw), BF),
+            V((half, tok, fb), BF),
+            V((half, tok, fb), BF),
             V((tok, width // 2), BF),
             dma((7,)),
+            dma((3,)), dma((3,)), pltpu.SemaphoreType.REGULAR,
             dma((3,)), dma((4,)),
-            dma((2 * ndp,)), dma((2 * ndp,)),
-            dma((ndp,)), dma((ndp,)),
+            dma((2, half)), dma((2, half)),
             dma((half,)), dma((half,)),
+            dma((chunks, half)), dma((chunks, half)),
+            dma((chunks, half)), dma((chunks, half)),
             dma((half,)), dma((half,)),
-            dma((half,)), dma((ndp,)), dma((half,)),
-            dma((ndp,)), dma((ndp,)),
             dma((2,)), dma((2,)),
         ],
         compiler_params=pltpu.CompilerParams(
@@ -641,12 +661,10 @@
         ),
     )(
         context_len,
-        depth,
-        cosine,
-        sine,
+        exit_depth,
         attn_gain,
-        mlp_gain.reshape(ndp, fb),
-        exit_hidden.reshape(tok, piece),
+        mlp_gain,
+        exit_hidden,
         w_query[0],
         w_keyval[0],
         kv_cache.reshape(reqs, ctx * n_kv, 128),
@@ -655,7 +673,7 @@
         w_up[0],
         w_down[0],
     )
-    return out.reshape(1, reqs, drafts, width // 2)
+    return out[None]
 
 
 def solution(mesh):

time: 122 us -> 97.5 us (0.80)
  Pallas kernels: 113 us -> 95.8 us
  local copies, waits for them, and re-layouts: 5.56 us -> 1.49 us
  other arithmetic: 2.85 us -> 0 us
    pallas_call x1, Pallas kernels: 113 us -> 95.8 us  [fused(): pl.pallas_call(functools.partial(fused_kernel, ndp), out_shape=jax.ShapeD...]
    reshape x3 -> x0, local copies, waits for them, and re-layouts: 3.49 us -> none  [the longest x1 1.5 us: fused(): return out.reshape(1, reqs, drafts, width // 2)]
    broadcast_in_dim x3 -> x0, local copies, waits for them, and re-layouts: 1.48 us -> none  [the longest x2 0.75 us: fused(): jnp.broadcast_to(jnp.repeat(exit_depth, drafts)[:, None], (tok, 128))]
    unnamed x1 -> x0, other arithmetic: 1.36 us -> none
where the time goes in v2:
time: 97.5 us; the launch traced here: 97.3 us
  Pallas kernels  95.8 us (98%)
  local copies, waits for them, and re-layouts  1.49 us (2%)
    pallas_call x1, Pallas kernels, fused(): pl.pallas_call(functools.partial(fused_kernel, ndp), out_shape=jax.ShapeD...  95.8 us

profile of v2, /device:TPU:3, one launch (start us, length us, event | category | flops | bytes accessed | tf_op | source)
XLA Modules:
  0.0 97.3 jit_solution(16143156243583960106)
XLA Ops:
  0.0 95.8 %shard_map.118 = bf16[8,4,1024]{2,1,0:T(4,128)(2,1)} custom-call(s32[8]{0:T(128)} %lens_ref.1, s32[8]{0:T(128)} %depth_ref.1, f32[1,2048]{1,0:T(1,128)} %gain_ref.1, f32[1,2048]{1,0:T(1,128)} %gain2_ref.1, bf16[8,4,512]{2,1,0:T(4,128)(2,1)} %entry_ref.1, bf16[2048,1024]{1,0:T(8,128)(2,1)} %bitcast.8, bf16[2048,512]{1,0:T(8,128)(2,1)} %bitcast.11, ...), custom_call_target="tpu_custom_call" | custom-call | tf_op jit(solution)/shard_map/pallas_call | solution.py:613
  95.8 1.5 %copy.14 = bf16[1,8,4,1024]{3,2,1,0:T(4,128)(2,1)} copy(bf16[1,8,4,1024]{3,2,1,0:T(4,128)(2,1)} %bitcast.15) | data formatting | bytes 131072

commit v3 on v2

--- a/solution.py
+++ b/solution.py
@@ -198,7 +198,7 @@
 
 
 MESH = pl.DeviceIdType.MESH
-CHUNKS = 2
+CHUNKS = 4
 BF = jnp.bfloat16
 F32 = jnp.float32
 
@@ -292,8 +292,11 @@
         )
 
     def twin_copy(k):
-        src, dst = [(wg_hbm, wg), (wu_hbm, wu), (wd_hbm, wd)][k]
-        return remote(src, dst.at[y], w_s.at[k], w_r.at[k], (s, t, twin))
+        if k == 2 * chunks:
+            return remote(wd_hbm, wd.at[y], w_s.at[k], w_r.at[k], (s, t, twin))
+        src, dst = [(wg_hbm, wg), (wu_hbm, wu)][k % 2]
+        cols = pl.ds(k // 2 * cw, cw)
+        return remote(src.at[:, cols], dst.at[y, :, cols], w_s.at[k], w_r.at[k], (s, t, twin))
 
     mine = s * 2 + t
     pending = []
@@ -306,7 +309,7 @@
 
     @pl.when(s == 0)
     def _():
-        for k in range(3):
+        for k in range(2 * chunks + 1):
             twin_copy(k).start()
 
     def permutation(transposed):
@@ -350,7 +353,7 @@
     @pl.when(s == 1)
     def _():
         pl.semaphore_wait(go, 1)
-        for k in range(3):
+        for k in range(2 * chunks + 1):
             twin_copy(k).start()
         for k in range(2):
             remote(res, cur.at[k], c_s.at[k], c_r.at[k], (0, k, d)).wait_recv()
@@ -471,16 +474,11 @@
 
     loads[4].wait()
     loads[5].wait()
-    for k in range(2):
-        twin_copy(k).wait()
-
-    @pl.when(s == 0)
-    def _():
-        pl.semaphore_signal(go, inc=1, device_id=(1, t, d), device_id_type=MESH)
-
     grid = xs[...].reshape(half * tok, fb)
     step = 512
     for c in range(chunks):
+        twin_copy(2 * c).wait()
+        twin_copy(2 * c + 1).wait()
         for i in range(cw // step):
             src = slice(c * cw + i * step, c * cw + (i + 1) * step)
             for g, w in enumerate((wg, wu)):
@@ -496,6 +494,13 @@
         sums = sums + sqr[b]
     scale = lax.rsqrt(jnp.sum(sums, axis=1, keepdims=True) * (1.0 / width) + EPS)
     for c in range(chunks):
+        if c == chunks - 1:
+            twin_copy(2 * chunks).wait()
+
+            @pl.when(s == 0)
+            def _():
+                pl.semaphore_signal(go, inc=1, device_id=(1, t, d), device_id_type=MESH)
+
         for zz in order:
             remote(zbuf.at[c, zz], zrec.at[c, zz], z_s.at[c, zz], z_r.at[c, zz], (s, t, zz * 2 + y)).wait_recv()
         for i in range(cw // step):
@@ -512,7 +517,6 @@
             remote(acts.at[c, z], acts.at[c, z], g_s.at[c, zz], g_r.at[c, z], (s, t, zz * 2 + y)).start()
 
     loads[6].wait()
-    twin_copy(2).wait()
     grown = None
     for c in range(chunks):
         for zz in order:
@@ -647,7 +651,7 @@
             V((half, tok, fb), BF),
             V((tok, width // 2), BF),
             dma((7,)),
-            dma((3,)), dma((3,)), pltpu.SemaphoreType.REGULAR,
+            dma((2 * chunks + 1,)), dma((2 * chunks + 1,)), pltpu.SemaphoreType.REGULAR,
             dma((3,)), dma((4,)),
             dma((2, half)), dma((2, half)),
             dma((half,)), dma((half,)),

time: 97.5 us -> 91.8 us (0.942)
  Pallas kernels: 95.8 us -> 89.4 us
    pallas_call x1, Pallas kernels: 95.8 us -> 89.4 us  [fused(): pl.pallas_call(functools.partial(fused_kernel, ndp), out_shape=jax.ShapeD...]
where the time goes in v3:
time: 91.8 us; the launch traced here: 90.9 us
  Pallas kernels  89.4 us (97%)
  local copies, waits for them, and re-layouts  1.49 us (2%)
    pallas_call x1, Pallas kernels, fused(): pl.pallas_call(functools.partial(fused_kernel, ndp), out_shape=jax.ShapeD...  89.4 us

profile of v3, /device:TPU:3, one launch (start us, length us, event | category | flops | bytes accessed | tf_op | source)
XLA Modules:
  0.0 90.9 jit_solution(9658543613791947194)
XLA Ops:
  0.0 89.4 %shard_map.118 = bf16[8,4,1024]{2,1,0:T(4,128)(2,1)} custom-call(s32[8]{0:T(128)} %lens_ref.1, s32[8]{0:T(128)} %depth_ref.1, f32[1,2048]{1,0:T(1,128)} %gain_ref.1, f32[1,2048]{1,0:T(1,128)} %gain2_ref.1, bf16[8,4,512]{2,1,0:T(4,128)(2,1)} %entry_ref.1, bf16[2048,1024]{1,0:T(8,128)(2,1)} %bitcast.8, bf16[2048,512]{1,0:T(8,128)(2,1)} %bitcast.11, ...), custom_call_target="tpu_custom_call" | custom-call | tf_op jit(solution)/shard_map/pallas_call | solution.py:617
  89.4 1.5 %copy.14 = bf16[1,8,4,1024]{3,2,1,0:T(4,128)(2,1)} copy(bf16[1,8,4,1024]{3,2,1,0:T(4,128)(2,1)} %bitcast.15) | data formatting | bytes 131072
